TPU v7x, 256 devices: a whole 4x4x8 slice. The times are simulated.
256 devices in a mesh: node: 64 (over y, z, core), feat: 4 (over x).
Axes of the slice: x: 4, y: 4, z: 8, core: 2. Of those that a mesh axis runs over, the one named last changes fastest.
Arguments:
- features: bfloat16 [32768, 128], P('node', 'feat'), may hold values from -10 to 10
- send_rows: int32 [64, 64, 64], P('node'), may hold values from 0 to 511
- send_count: int32 [64, 64], P('node'), may hold values from 1 to 64, 2048 in all within a row
- tile_src: int32 [256, 16], P('node'), may hold values from 0 to 35
- tile_val: bfloat16 [256, 16, 128, 128], P('node'), may hold values from 0 to 0.0009765625
- labels: int32 [32768], P('node'), may hold values from 0 to 171
- w_self1: bfloat16 [128, 1024], P('feat'), may hold values from -0.5 to 0.5
- w_neigh1: bfloat16 [128, 1024], P('feat'), may hold values from -0.5 to 0.5
- w_self2: bfloat16 [1024, 172], P('feat'), may hold values from -0.5 to 0.5
- w_neigh2: bfloat16 [1024, 172], P('feat'), may hold values from -0.1875 to 0.1875
Outputs:
- mean_loss: float32 [], replicated
- grad_self1: float32 [128, 1024], P('feat')
- grad_neigh1: float32 [128, 1024], P('feat')
- grad_self2: float32 [1024, 172], P('feat')
- grad_neigh2: float32 [1024, 172], P('feat')
Inputs may be any that keep to these rules, and one draw needn't show every extreme that they name: `send_rows`: row indices within the sending partition's 512 rows. Each row of send_count sums to 2048 and holds 64 at least once. `tile_src`: block numbers of the destination partition's source rows: numbers below 4 name its own rows, the others its halo slots.
All inputs are finite; a program needn't handle non-finite values.
Results may differ from a plain program's by a relative error of at most 0.00095.
The roundings to bfloat16 on the way count: a program that leaves them out, or rounds other values in their place, can miss the bound.
Values may be sent and summed in bfloat16 or wider, within the bound.
A program may use at most 64 MiB of HBM per device.

v0:
```python
import math
import jax
import jax.numpy as jnp
from jax import lax
from jax.sharding import PartitionSpec as P


def pack_rows(own_rows, send_rows, send_count):
    slot_total = send_rows.shape[2]
    picked = jnp.take(own_rows, send_rows[0].reshape(-1), axis=0)
    picked = picked.reshape(send_rows.shape[1], slot_total, own_rows.shape[1])
    in_use = jnp.arange(slot_total, dtype=jnp.int32)[None, :] < send_count[0][:, None]
    return jnp.where(in_use[:, :, None], picked, jnp.zeros_like(picked))


def aggregate(own_rows, arrived, tile_src, tile_val):
    col_count = own_rows.shape[1]
    blocks = jnp.concatenate([own_rows, arrived], axis=0).reshape(-1, 128, col_count)
    chosen = jnp.take(blocks, tile_src, axis=0)
    summed = jnp.einsum("bkij,bkjh->bih", tile_val, chosen, preferred_element_type=jnp.float32)
    return summed.reshape(own_rows.shape[0], col_count).astype(jnp.bfloat16)


def spread_back(grads, tile_src, tile_val, src_total):
    col_count = grads.shape[1]
    per_tile = jnp.einsum(
        "bkij,bih->bkjh",
        tile_val,
        grads.reshape(-1, 128, col_count),
        preferred_element_type=jnp.float32,
    )
    one_hot = (
        tile_src.reshape(-1)[None, :] == jnp.arange(src_total // 128, dtype=jnp.int32)[:, None]
    ).astype(jnp.float32)
    landed = jnp.dot(
        one_hot,
        per_tile.reshape(one_hot.shape[1], -1),
        precision=lax.Precision.HIGHEST,
        preferred_element_type=jnp.float32,
    )
    return landed.reshape(src_total, col_count)


def cross_entropy(logits, labels, grad_scale):
    row_max = jnp.max(logits, axis=1, keepdims=True)
    shifted = logits - row_max
    total_exp = jnp.sum(jnp.exp(shifted), axis=1, keepdims=True)
    classes = jnp.arange(logits.shape[1], dtype=jnp.int32)
    target = (labels[:, None] == classes[None, :]).astype(jnp.float32)
    row_loss = jnp.log(total_exp)[:, 0] - jnp.sum(shifted * target, axis=1)
    grads = ((jnp.exp(shifted) / total_exp - target) * grad_scale).astype(jnp.bfloat16)
    return (row_loss, grads)


def shards(
    features,
    send_rows,
    send_count,
    tile_src,
    tile_val,
    labels,
    w_self1,
    w_neigh1,
    w_self2,
    w_neigh2,
):
    node_count = lax.axis_size("node")
    own_count = features.shape[0]
    slot_total = send_rows.shape[2]
    src_total = own_count + node_count * slot_total
    node_total = own_count * node_count
    grad_scale = 1.0 / math.sqrt(node_total)
    outgoing = pack_rows(features, send_rows, send_count)
    arrived = lax.all_to_all(outgoing, "node", split_axis=0, concat_axis=0, tiled=True).reshape(
        -1, features.shape[1]
    )
    agg_one = aggregate(features, arrived, tile_src, tile_val)
    partial_one = jnp.dot(features, w_self1, preferred_element_type=jnp.float32)
    partial_one = partial_one + jnp.dot(agg_one, w_neigh1, preferred_element_type=jnp.float32)
    pre_act = lax.psum_scatter(partial_one, "feat", scatter_dimension=1, tiled=True)
    activated, pullback = jax.vjp(lambda inner: jax.nn.gelu(inner, approximate=True), pre_act)
    hidden = activated.astype(jnp.bfloat16)
    unit_count = hidden.shape[1]
    outgoing_two = pack_rows(hidden, send_rows, send_count)
    arrived_two = lax.all_to_all(
        outgoing_two, "node", split_axis=0, concat_axis=0, tiled=True
    ).reshape(-1, unit_count)
    agg_two = aggregate(hidden, arrived_two, tile_src, tile_val)
    partial_two = jnp.dot(hidden, w_self2, preferred_element_type=jnp.float32)
    partial_two = partial_two + jnp.dot(agg_two, w_neigh2, preferred_element_type=jnp.float32)
    logits = lax.psum(partial_two, "feat")
    row_loss, dlogits = cross_entropy(logits, labels, grad_scale)
    mean_loss = lax.psum(jnp.sum(row_loss), "node") / node_total
    grad_pair = lax.psum(
        (
            jnp.einsum("nh,nc->hc", hidden, dlogits, preferred_element_type=jnp.float32),
            jnp.einsum("nh,nc->hc", agg_two, dlogits, preferred_element_type=jnp.float32),
        ),
        "node",
    )
    back_grad = jnp.einsum(
        "nc,hc->nh", dlogits, w_neigh2, preferred_element_type=jnp.float32
    ).astype(jnp.bfloat16)
    direct = jnp.einsum("nc,hc->nh", dlogits, w_self2, preferred_element_type=jnp.float32)
    landed = spread_back(back_grad, tile_src, tile_val, src_total)
    halo_back = landed[own_count:].reshape(node_count, slot_total, unit_count)
    returned = lax.all_to_all(
        halo_back.astype(jnp.bfloat16), "node", split_axis=0, concat_axis=0, tiled=True
    ).astype(halo_back.dtype)
    in_use = jnp.arange(slot_total, dtype=jnp.int32)[None, :] < send_count[0][:, None]
    returned = jnp.where(in_use[:, :, None], returned, jnp.zeros_like(returned))
    back_rows = jax.ops.segment_sum(
        returned.reshape(-1, unit_count), send_rows[0].reshape(-1), num_segments=own_count
    )
    back_hidden = direct + landed[:own_count] + back_rows
    pre_grad = pullback(back_hidden)[0].astype(jnp.bfloat16)
    shard_piece = lax.all_gather(pre_grad, "feat", axis=1, tiled=True)
    local_grads = jnp.stack(
        [
            jnp.einsum("nf,nh->fh", features, shard_piece, preferred_element_type=jnp.float32),
            jnp.einsum("nf,nh->fh", agg_one, shard_piece, preferred_element_type=jnp.float32),
        ]
    )
    summed = lax.psum(local_grads, "node")
    return (mean_loss, summed[0], summed[1], grad_pair[0], grad_pair[1])


def solution(mesh):
    in_specs = (
        P("node", "feat"),
        P("node", None, None),
        P("node", None),
        P("node", None),
        P("node", None, None, None),
        P("node"),
        P("feat", None),
        P("feat", None),
        P("feat", None),
        P("feat", None),
    )
    out_specs = (P(), P("feat", None), P("feat", None), P("feat", None), P("feat", None))
    return jax.shard_map(shards, mesh=mesh, in_specs=in_specs, out_specs=out_specs, check_vma=False)
```

profile of v0, /device:TPU:2, one launch (start us, length us, event | category | flops | bytes accessed | tf_op | source)
XLA Modules:
  0.0 571.0 jit_solution(3139560621322994043)
XLA Ops:
  7.2 1.0 reshape_squeeze.7
  8.2 0.9 iota_compare_fusion.1
  9.1 0.9 copy.35
  10.0 12.1 %gather_fusion = bf16[4096,32]{1,0:T(8,128)(2,1)S(1)} fusion(bf16[512,32]{1,0:T(8,128)(2,1)S(1)} %copy.35, s32[4096]{0:T(1024)S(1)} %broadcast_clamp_fusion), kind=kCustom, calls=%fused_computation | custom fusion | bytes 540672 | tf_op jit(solution)/shard_map/jit(_take)/gather | solution.py:10
  22.1 1.1 copy.36
  23.3 1.2 fusion.30
  24.4 1.0 reshape.178
  25.4 12.1 %all-to-all-start = ((bf16[64,2,1024]{2,1,0:T(2,128)(2,1)}), bf16[64,2,1024]{2,1,0:T(2,128)(2,1)S(1)}, u32[]{:S(2)}, u32[]{:S(2)}) async-start(bf16[64,2,1024]{2,1,0:T(2,128)(2,1)} %reshape.178), calls=%async_computation | async-start | bytes 524288 | tf_op jit(solution)/shard_map/all_to_all | solution.py:74
  37.5 0.0 reduce-scatter.2.cloned.1.call-start
  37.6 0.1 reshape.140
  37.7 1.8 fusion.31
  39.5 10.0 %all-to-all-done = bf16[64,2,1024]{2,1,0:T(2,128)(2,1)S(1)} async-done(((bf16[64,2,1024]{2,1,0:T(2,128)(2,1)}), bf16[64,2,1024]{2,1,0:T(2,128)(2,1)S(1)}, u32[]{:S(2)}, u32[]{:S(2)}) %all-to-all-start) | async-done | bytes 262176 | tf_op jit(solution)/shard_map/all_to_all | solution.py:74
  49.5 0.3 reshape.179
  49.9 0.2 copy.37
  50.1 0.5 reshape.123
  50.6 0.1 copy_bitcast_fusion
  50.6 0.7 gather_fusion.1
  51.3 0.8 fusion.11
  52.1 0.7 copy-done.3
  52.9 1.8 convolution_add_fusion
  54.7 28.0 %reduce-scatter.2.cloned.1.call-done = f32[512,256]{1,0:T(8,128)} async-done(((f32[512,1024]{1,0:T(8,128)}), f32[512,256]{1,0:T(8,128)}) %reduce-scatter.2.cloned.1.call-update) | async-done | bytes 524304 | tf_op jit(solution)/shard_map/reduce_scatter | solution.py:80
  82.7 1.2 multiply_convert_fusion
  83.9 16.9 %gather_fusion.2 = bf16[4096,256]{1,0:T(8,128)(2,1)} fusion(bf16[512,256]{1,0:T(8,128)(2,1)S(1)} %multiply_convert_fusion, s32[4096]{0:T(1024)S(1)} %broadcast_clamp_fusion), kind=kCustom, calls=%fused_computation.2 | custom fusion | bytes 4210688 | tf_op jit(solution)/shard_map/jit(_take)/gather | solution.py:10
  100.8 4.4 select_select_fusion
  105.2 10.9 %all-to-all-start.1 = ((bf16[64,64,256]{2,1,0:T(8,128)(2,1)}), bf16[64,64,256]{2,1,0:T(8,128)(2,1)}, u32[]{:S(2)}, u32[]{:S(2)}) async-start(bf16[64,64,256]{2,1,0:T(8,128)(2,1)} %select_select_fusion), calls=%async_computation.2 | async-start | bytes 4194304 | tf_op jit(solution)/shard_map/all_to_all | solution.py:85
  116.1 0.2 fusion.32
  116.4 50.7 %all-to-all-done.1 = bf16[64,64,256]{2,1,0:T(8,128)(2,1)} async-done(((bf16[64,64,256]{2,1,0:T(8,128)(2,1)}), bf16[64,64,256]{2,1,0:T(8,128)(2,1)}, u32[]{:S(2)}, u32[]{:S(2)}) %all-to-all-start.1) | async-done | bytes 2097184 | tf_op jit(solution)/shard_map/all_to_all | solution.py:85
  167.1 3.2 pad_maximum_fusion
  170.3 4.4 gather_fusion.3
  174.7 3.2 fusion.7
  178.0 1.0 convolution_add_fusion.2
  179.0 0.1 eq.31
  179.0 42.6 %all-reduce.4.cloned.1.call-done = f32[512,172]{0,1:T(8,128)} async-done(((f32[512,172]{0,1:T(8,128)}), f32[512,172]{0,1:T(8,128)}) %all-reduce.4.cloned.1.call-update) | async-done | bytes 352272 | tf_op jit(solution)/shard_map/psum | solution.py:91
  221.7 1.0 reduce_max.9
  222.7 1.1 exponential_reduce_fusion
  223.8 1.1 multiply_convert_fusion.1
  224.9 0.3 convolution_convert_fusion
  225.2 4.5 convolution_bitcast_fusion
  229.7 8.7 %copy.41 = f32[4,16,128,256]{3,2,1,0:T(8,128)} copy(f32[4,16,128,256]{2,3,1,0:T(8,128)} %convolution_bitcast_fusion) | data formatting | bytes 16777216 | tf_op jit(solution)/shard_map/bkij,bih->bkjh/dot_general | solution.py:26
  238.4 8.1 %copy.49 = f32[8,8,128,256]{3,1,2,0:T(8,128)S(1)} copy(f32[8,8,128,256]{3,2,1,0:T(8,128)} %bitcast.90) | data formatting | bytes 16777216
  246.5 4.3 fusion.26
  250.8 2.3 copy-done.2
  253.1 0.3 slice.37
  253.4 2.4 convert_element_type.51
  255.9 10.9 %all-to-all-start.2 = ((bf16[64,64,256]{2,1,0:T(8,128)(2,1)}), bf16[64,64,256]{2,1,0:T(8,128)(2,1)}, u32[]{:S(2)}, u32[]{:S(2)}) async-start(bf16[64,64,256]{2,1,0:T(8,128)(2,1)} %convert_element_type.51), calls=%async_computation.3 | async-start | bytes 4194304 | tf_op jit(solution)/shard_map/all_to_all | solution.py:107
  266.8 0.1 reshape.164
  266.9 0.4 slice.18
  267.2 0.3 convolution_add_fusion.1
  267.5 50.3 %all-to-all-done.2 = bf16[64,64,256]{2,1,0:T(8,128)(2,1)} async-done(((bf16[64,64,256]{2,1,0:T(8,128)(2,1)}), bf16[64,64,256]{2,1,0:T(8,128)(2,1)}, u32[]{:S(2)}, u32[]{:S(2)}) %all-to-all-start.2) | async-done | bytes 2097184 | tf_op jit(solution)/shard_map/all_to_all | solution.py:107
  317.8 3.5 convert_select_fusion
  321.3 23.3 %scatter_fusion = f32[512,256]{1,0:T(8,128)S(1)} fusion(f32[512,256]{1,0:T(8,128)S(1)} %convolution_add_fusion.1, s32[4096]{0:T(1024)S(1)} %reshape.164, f32[4096,256]{1,0:T(8,128)} %bitcast.92), kind=kCustom, calls=%fused_computation.4 | custom fusion | flops 1048576 | bytes 12599296 | tf_op jit(solution)/shard_map/scatter-add | solution.py:112
  344.6 1.1 fusion.18
  345.7 0.9 fusion.34
  346.6 0.9 fusion.33
  347.5 23.0 %all-gather.2.cloned.1.call-done = bf16[512,1024]{1,0:T(8,128)(2,1)} async-done(((bf16[512,256]{1,0:T(8,128)(2,1)}), bf16[512,1024]{1,0:T(8,128)(2,1)}) %all-gather.2.cloned.1.call-update) | async-done | bytes 1048592 | tf_op jit(solution)/shard_map/all_gather | solution.py:117
  370.5 1.7 convolution_bitcast_fusion.2
  372.2 1.5 convolution_bitcast_fusion.1
  373.7 0.7 pad_maximum_fusion.1
  374.4 0.6 subtract_reduce_fusion
  375.0 128.7 %psum.36 = f32[]{:T(128)} all-reduce(f32[]{:T(128)} %subtract_reduce_fusion), channel_id=1, replica_groups=mesh['node'=64,'feat'=4] {'node'}, use_global_device_ids=true, to_apply=%region_6.7 | all-reduce | flops 1 | bytes 8 | tf_op jit(solution)/shard_map/psum | solution.py:93
  504.4 54.0 %all-reduce.6.cloned.1.call-done = (f32[2,32,1024]{2,1,0:T(8,128)}, f32[256,172]{0,1:T(8,128)}, f32[256,172]{0,1:T(8,128)}) async-done(((f32[2,32,1024]{2,1,0:T(8,128)}, f32[256,172]{0,1:T(8,128)}, f32[256,172]{0,1:T(8,128)}), (f32[2,32,1024]{2,1,0:T(8,128)}, f32[256,172]{0,1:T(8,128)}, f32[256,172]{0,1:T(8,128)})) %all-reduce.6.cloned.1.call-update) | async-done | bytes 614416 | tf_op jit(solution)/shard_map/psum | solution.py:124
  558.4 1.7 slice_bitcast_fusion
  560.1 1.6 copy.64
  561.7 1.6 copy.65
  (38 shorter events, 0.3 us)
Async XLA Ops:
  7.2 44.1 %copy-start = (bf16[4,16,128,128]{3,2,1,0:T(8,128)(2,1)S(1)}, bf16[4,16,128,128]{3,2,1,0:T(8,128)(2,1)}, u32[]{:S(2)}) copy-start(bf16[4,16,128,128]{3,2,1,0:T(8,128)(2,1)} %param.14) | copy-start | bytes 6291460
  22.1 15.5 %copy-start.11 = (s32[4,16]{1,0:T(4,128)S(1)}, s32[4,16]{1,0:T(4,128)}, u32[]{:S(2)}) copy-start(s32[4,16]{1,0:T(4,128)} %param.13) | copy-start | bytes 772
  22.1 15.6 %copy-start.5 = (bf16[512,32]{0,1:T(8,128)(2,1)S(1)}, bf16[512,32]{0,1:T(8,128)(2,1)}, u32[]{:S(2)}) copy-start(bf16[512,32]{0,1:T(8,128)(2,1)} %param.10) | copy-start | bytes 98308
  22.1 15.6 %copy-start.10 = (bf16[32,1024]{1,0:T(8,128)(2,1)S(1)}, bf16[32,1024]{1,0:T(8,128)(2,1)}, u32[]{:S(2)}) copy-start(bf16[32,1024]{1,0:T(8,128)(2,1)} %param.16) | copy-start | bytes 196612
  25.4 24.1 %all-to-all-start = ((bf16[64,2,1024]{2,1,0:T(2,128)(2,1)}), bf16[64,2,1024]{2,1,0:T(2,128)(2,1)S(1)}, u32[]{:S(2)}, u32[]{:S(2)}) async-start(bf16[64,2,1024]{2,1,0:T(2,128)(2,1)} %reshape.178), calls=%async_computation | async-start | bytes 524288 | tf_op jit(solution)/shard_map/all_to_all | solution.py:74
  37.5 45.1 %reduce-scatter.2.cloned.1.call-start = ((), (), s32[]{:S(2)}) async-start(), calls=%async_computation.4 | async-start | bytes 2621440 | tf_op jit(solution)/shard_map/reduce_scatter | solution.py:80
  51.3 1.6 copy-start.3
  51.3 1.6 copy-start.9
  105.2 10.9 %copy-start.7 = (bf16[256,172]{0,1:T(8,128)(2,1)S(1)}, bf16[256,172]{0,1:T(8,128)(2,1)}, u32[]{:S(2)}) copy-start(bf16[256,172]{0,1:T(8,128)(2,1)} %param.18) | copy-start | bytes 264196
  105.2 61.9 %all-to-all-start.1 = ((bf16[64,64,256]{2,1,0:T(8,128)(2,1)}), bf16[64,64,256]{2,1,0:T(8,128)(2,1)}, u32[]{:S(2)}, u32[]{:S(2)}) async-start(bf16[64,64,256]{2,1,0:T(8,128)(2,1)} %select_select_fusion), calls=%async_computation.2 | async-start | bytes 4194304 | tf_op jit(solution)/shard_map/all_to_all | solution.py:85
  116.1 105.6 %all-reduce.4.cloned.1.call-start = ((), (), s32[]{:S(2)}) async-start(), calls=%async_computation.5 | async-start | bytes 720896 | tf_op jit(solution)/shard_map/psum | solution.py:91
  174.7 3.2 copy-start.6
  174.7 48.0 %copy-start.12 = (s32[512]{0:T(512)S(1)}, s32[512]{0:T(512)}, u32[]{:S(2)}) copy-start(s32[512]{0:T(512)} %param.15) | copy-start | bytes 6148
  250.8 2.3 copy-start.2
  255.9 10.9 %copy-start.8 = (s32[1,64,64]{2,1,0:T(8,128)S(1)}, s32[1,64,64]{2,1,0:T(8,128)}, u32[]{:S(2)}) copy-start(s32[1,64,64]{2,1,0:T(8,128)} %param.11) | copy-start | bytes 49156
  255.9 11.0 %slice-start = ((f32[36,32768]{1,0:T(8,128)}), f32[4,32768]{1,0:T(4,128)S(1)}, s32[]{:S(2)}) async-start(f32[36,32768]{1,0:T(8,128)} %copy-done.2), calls=%async_computation.8 | async-start | bytes 1048576 | tf_op jit(solution)/shard_map/slice | solution.py:115
  255.9 61.9 %all-to-all-start.2 = ((bf16[64,64,256]{2,1,0:T(8,128)(2,1)}), bf16[64,64,256]{2,1,0:T(8,128)(2,1)}, u32[]{:S(2)}, u32[]{:S(2)}) async-start(bf16[64,64,256]{2,1,0:T(8,128)(2,1)} %convert_element_type.51), calls=%async_computation.3 | async-start | bytes 4194304 | tf_op jit(solution)/shard_map/all_to_all | solution.py:107
  266.7 103.8 %all-gather.2.cloned.1.call-start = ((), (), s32[]{:S(2)}) async-start(), calls=%async_computation.6 | async-start | bytes 1310720 | tf_op jit(solution)/shard_map/all_gather | solution.py:117
  321.3 23.3 %copy-start.4 = (f32[512,256]{1,0:T(8,128)S(1)}, f32[512,256]{1,0:T(8,128)}, u32[]{:S(2)}) copy-start(f32[512,256]{1,0:T(8,128)} %reduce-scatter.2.cloned.1.call-done) | copy-start | bytes 1572868
  345.7 212.8 %all-reduce.6.cloned.1.call-start = ((), (), s32[]{:S(2)}) async-start(), calls=%async_computation.7 | async-start | bytes 1245184 | tf_op jit(solution)/shard_map/psum | solution.py:124
  370.5 192.8 %copy-start.1 = (bf16[4,16,128,128]{3,2,1,0:T(8,128)(2,1)S(1)}, bf16[4,16,128,128]{3,2,1,0:T(8,128)(2,1)}, u32[]{:S(2)}) copy-start(bf16[4,16,128,128]{3,2,1,0:T(8,128)(2,1)} %param.14) | copy-start | bytes 6291460
Sparse Core Ops, SparseCore 0:
  54.8 27.8 reduce-scatter.1
  179.1 42.5 all-reduce.3
  345.8 24.6 all-gather.1
  375.2 183.2 all-reduce.5
where the time goes:
time: 572 us; the launch traced here: 571 us
  waiting for transfers between devices  259 us (45%)
  blocking collectives  129 us (23%)
  local copies, waits for them, and re-layouts  67.3 us (12%)
  other arithmetic  43.3 us (8%)
  starting transfers between devices  34 us (6%)
  matrix products  23.1 us (4%)
  between operations  15.8 us (3%)
    psum x1, blocking collectives, shards(): mean_loss = lax.psum(jnp.sum(row_loss), 'node') / node_total  129 us
    psum x1, waiting for transfers between devices, shards(): summed = lax.psum(local_grads, 'node')  54 us
    all_to_all x1, waiting for transfers between devices, shards(): lax.all_to_all(outgoing_two, 'node', split_axis=0, concat_axis=0, tiled=T...  50.7 us
    all_to_all x1, waiting for transfers between devices, shards(): lax.all_to_all(halo_back.astype(jnp.bfloat16), 'node', split_axis=0, conc...  50.3 us
    psum x1, waiting for transfers between devices, shards(): logits = lax.psum(partial_two, 'feat')  42.6 us
    gather x3, local copies, waits for them, and re-layouts, pack_rows(): picked = jnp.take(own_rows, send_rows[0].reshape(-1), axis=0)  30.2 us
    reduce_scatter x1, waiting for transfers between devices, shards(): lax.psum_scatter(partial_one, 'feat', scatter_dimension=1, tiled=True)  28 us
    scatter-add x1, other arithmetic, shards(): jax.ops.segment_sum(returned.reshape(-1, unit_count), send_rows[0].reshap...  23.3 us
  transfers between devices with their start and end apart: 7, of which 7 were waited for; matrix products, arithmetic and copies ran while one was open for 1% of the time, Pallas kernels for 0%

commit v1 on v0

--- a/solution.py
+++ b/solution.py
@@ -3,6 +3,19 @@
 import jax.numpy as jnp
 from jax import lax
 from jax.sharding import PartitionSpec as P
+
+
+def collect(array, axis, dim):
+    ways = lax.axis_size(axis)
+    up = [(d, (d + 1) % ways) for d in range(ways)]
+    down = [(d, (d - 1) % ways) for d in range(ways)]
+    earlier, later = ([array], [array])
+    for _ in range(ways // 2):
+        earlier.append(lax.ppermute(earlier[-1], axis, up))
+    for _ in range((ways - 1) // 2):
+        later.append(lax.ppermute(later[-1], axis, down))
+    line = jnp.concatenate([*earlier[::-1], *later[1:]], axis=dim)
+    return jnp.roll(line, (lax.axis_index(axis) - ways // 2) * array.shape[dim], axis=dim)
 
 
 def pack_rows(own_rows, send_rows, send_count):
@@ -114,7 +127,7 @@
     )
     back_hidden = direct + landed[:own_count] + back_rows
     pre_grad = pullback(back_hidden)[0].astype(jnp.bfloat16)
-    shard_piece = lax.all_gather(pre_grad, "feat", axis=1, tiled=True)
+    shard_piece = collect(pre_grad, "feat", 1)
     local_grads = jnp.stack(
         [
             jnp.einsum("nf,nh->fh", features, shard_piece, preferred_element_type=jnp.float32),

time: 572 us -> 560 us (0.979)
  waiting for transfers between devices: 259 us -> 249 us
    all_gather x1 -> x0, waiting for transfers between devices: 23 us -> none  [shards(): shard_piece = lax.all_gather(pre_grad, 'feat', axis=1, tiled=True)]
    ppermute x0 -> x3, waiting for transfers between devices: none -> 12.6 us  [the longest x2 10.6 us: collect(): earlier.append(lax.ppermute(earlier[-1], axis, up))]
    unnamed x32 -> x39, local copies, waits for them, and re-layouts: 16.6 us -> 16.8 us
  transfers between devices with their start and end apart: 7 -> 9, of which waited for: 7 -> 9; matrix products, arithmetic and copies ran while one was open for 1% -> 1% of each run, Pallas kernels for 0% -> 0%
where the time goes in v1:
time: 560 us; the launch traced here: 559 us
  waiting for transfers between devices  249 us (44%)
  blocking collectives  125 us (22%)
  local copies, waits for them, and re-layouts  67.5 us (12%)
  other arithmetic  42.6 us (8%)
  starting transfers between devices  38.5 us (7%)
  matrix products  20.5 us (4%)
  between operations  15.9 us (3%)
    psum x1, blocking collectives, shards(): mean_loss = lax.psum(jnp.sum(row_loss), 'node') / node_total  125 us
    psum x1, waiting for transfers between devices, shards(): summed = lax.psum(local_grads, 'node')  54.8 us
    all_to_all x1, waiting for transfers between devices, shards(): lax.all_to_all(outgoing_two, 'node', split_axis=0, concat_axis=0, tiled=T...  50.7 us
    all_to_all x1, waiting for transfers between devices, shards(): lax.all_to_all(halo_back.astype(jnp.bfloat16), 'node', split_axis=0, conc...  50.3 us
    psum x1, waiting for transfers between devices, shards(): logits = lax.psum(partial_two, 'feat')  42.6 us
    gather x3, local copies, waits for them, and re-layouts, pack_rows(): picked = jnp.take(own_rows, send_rows[0].reshape(-1), axis=0)  30.2 us
    reduce_scatter x1, waiting for transfers between devices, shards(): lax.psum_scatter(partial_one, 'feat', scatter_dimension=1, tiled=True)  28 us
    scatter-add x1, other arithmetic, shards(): jax.ops.segment_sum(returned.reshape(-1, unit_count), send_rows[0].reshap...  23.3 us
  transfers between devices with their start and end apart: 9, of which 9 were waited for; matrix products, arithmetic and copies ran while one was open for 1% of the time, Pallas kernels for 0%

profile of v1, /device:TPU:2, one launch (start us, length us, event | category | flops | bytes accessed | tf_op | source)
XLA Modules:
  0.0 559.0 jit_solution(7393468102264012531)
XLA Ops:
  7.2 1.0 reshape_squeeze.7
  8.2 0.9 iota_compare_fusion.1
  9.1 0.9 copy.35
  10.0 12.1 %gather_fusion = bf16[4096,32]{1,0:T(8,128)(2,1)S(1)} fusion(bf16[512,32]{1,0:T(8,128)(2,1)S(1)} %copy.35, s32[4096]{0:T(1024)S(1)} %broadcast_clamp_fusion), kind=kCustom, calls=%fused_computation | custom fusion | bytes 540672 | tf_op jit(solution)/shard_map/jit(_take)/gather | solution.py:23
  22.1 1.1 copy.36
  23.3 1.2 fusion.34
  24.4 1.0 reshape.178
  25.4 12.1 %all-to-all-start = ((bf16[64,2,1024]{2,1,0:T(2,128)(2,1)}), bf16[64,2,1024]{2,1,0:T(2,128)(2,1)S(1)}, u32[]{:S(2)}, u32[]{:S(2)}) async-start(bf16[64,2,1024]{2,1,0:T(2,128)(2,1)} %reshape.178), calls=%async_computation | async-start | bytes 524288 | tf_op jit(solution)/shard_map/all_to_all | solution.py:87
  37.7 1.8 fusion.35
  39.5 10.0 %all-to-all-done = bf16[64,2,1024]{2,1,0:T(2,128)(2,1)S(1)} async-done(((bf16[64,2,1024]{2,1,0:T(2,128)(2,1)}), bf16[64,2,1024]{2,1,0:T(2,128)(2,1)S(1)}, u32[]{:S(2)}, u32[]{:S(2)}) %all-to-all-start) | async-done | bytes 262176 | tf_op jit(solution)/shard_map/all_to_all | solution.py:87
  49.5 0.3 reshape.179
  49.9 0.2 copy.37
  50.1 0.5 reshape.123
  50.6 0.7 gather_fusion.1
  51.3 0.8 fusion.11
  52.1 0.7 copy-done.3
  52.9 1.8 convolution_add_fusion
  54.7 28.0 %reduce-scatter.2.cloned.1.call-done = f32[512,256]{1,0:T(8,128)} async-done(((f32[512,1024]{1,0:T(8,128)}), f32[512,256]{1,0:T(8,128)}) %reduce-scatter.2.cloned.1.call-update) | async-done | bytes 524304 | tf_op jit(solution)/shard_map/reduce_scatter | solution.py:93
  82.7 1.2 multiply_convert_fusion
  83.9 16.9 %gather_fusion.2 = bf16[4096,256]{1,0:T(8,128)(2,1)} fusion(bf16[512,256]{1,0:T(8,128)(2,1)S(1)} %multiply_convert_fusion, s32[4096]{0:T(1024)S(1)} %broadcast_clamp_fusion), kind=kCustom, calls=%fused_computation.2 | custom fusion | bytes 4210688 | tf_op jit(solution)/shard_map/jit(_take)/gather | solution.py:23
  100.8 4.4 select_select_fusion
  105.2 10.9 %all-to-all-start.1 = ((bf16[64,64,256]{2,1,0:T(8,128)(2,1)}), bf16[64,64,256]{2,1,0:T(8,128)(2,1)}, u32[]{:S(2)}, u32[]{:S(2)}) async-start(bf16[64,64,256]{2,1,0:T(8,128)(2,1)} %select_select_fusion), calls=%async_computation.2 | async-start | bytes 4194304 | tf_op jit(solution)/shard_map/all_to_all | solution.py:98
  116.1 0.2 fusion.36
  116.4 50.7 %all-to-all-done.1 = bf16[64,64,256]{2,1,0:T(8,128)(2,1)} async-done(((bf16[64,64,256]{2,1,0:T(8,128)(2,1)}), bf16[64,64,256]{2,1,0:T(8,128)(2,1)}, u32[]{:S(2)}, u32[]{:S(2)}) %all-to-all-start.1) | async-done | bytes 2097184 | tf_op jit(solution)/shard_map/all_to_all | solution.py:98
  167.1 3.2 pad_maximum_fusion
  170.3 4.4 gather_fusion.3
  174.7 3.2 fusion.7
  178.0 1.0 convolution_add_fusion.2
  179.0 42.6 %all-reduce.4.cloned.1.call-done = f32[512,172]{0,1:T(8,128)} async-done(((f32[512,172]{0,1:T(8,128)}), f32[512,172]{0,1:T(8,128)}) %all-reduce.4.cloned.1.call-update) | async-done | bytes 352272 | tf_op jit(solution)/shard_map/psum | solution.py:104
  221.7 1.0 reduce_max.9
  222.7 1.1 exponential_reduce_fusion
  223.8 1.1 multiply_convert_fusion.1
  224.9 0.3 convolution_convert_fusion
  225.2 4.5 convolution_bitcast_fusion
  229.7 8.7 %copy.41 = f32[4,16,128,256]{3,2,1,0:T(8,128)} copy(f32[4,16,128,256]{2,3,1,0:T(8,128)} %convolution_bitcast_fusion) | data formatting | bytes 16777216 | tf_op jit(solution)/shard_map/bkij,bih->bkjh/dot_general | solution.py:39
  238.4 8.1 %copy.49 = f32[8,8,128,256]{3,1,2,0:T(8,128)S(1)} copy(f32[8,8,128,256]{3,2,1,0:T(8,128)} %bitcast.88) | data formatting | bytes 16777216
  246.5 4.3 fusion.28
  250.8 2.3 copy-done.2
  253.1 0.3 slice.37
  253.4 2.4 convert_element_type.51
  255.9 10.9 %all-to-all-start.2 = ((bf16[64,64,256]{2,1,0:T(8,128)(2,1)}), bf16[64,64,256]{2,1,0:T(8,128)(2,1)}, u32[]{:S(2)}, u32[]{:S(2)}) async-start(bf16[64,64,256]{2,1,0:T(8,128)(2,1)} %convert_element_type.51), calls=%async_computation.3 | async-start | bytes 4194304 | tf_op jit(solution)/shard_map/all_to_all | solution.py:120
  266.9 0.4 slice.18
  267.2 0.3 convolution_add_fusion.1
  267.5 50.3 %all-to-all-done.2 = bf16[64,64,256]{2,1,0:T(8,128)(2,1)} async-done(((bf16[64,64,256]{2,1,0:T(8,128)(2,1)}), bf16[64,64,256]{2,1,0:T(8,128)(2,1)}, u32[]{:S(2)}, u32[]{:S(2)}) %all-to-all-start.2) | async-done | bytes 2097184 | tf_op jit(solution)/shard_map/all_to_all | solution.py:120
  317.8 3.5 convert_select_fusion
  321.3 23.3 %scatter_fusion = f32[512,256]{1,0:T(8,128)S(1)} fusion(f32[512,256]{1,0:T(8,128)S(1)} %convolution_add_fusion.1, s32[4096]{0:T(1024)S(1)} %reshape.164, f32[4096,256]{1,0:T(8,128)} %bitcast.90), kind=kCustom, calls=%fused_computation.4 | custom fusion | flops 1048576 | bytes 12599296 | tf_op jit(solution)/shard_map/scatter-add | solution.py:125
  344.6 0.4 fusion.20
  345.0 1.8 collective-permute-start
  346.8 6.6 %collective-permute-done = bf16[512,256]{1,0:T(8,128)(2,1)S(1)} collective-permute-done((bf16[512,256]{1,0:T(8,128)(2,1)S(1)}, bf16[512,256]{1,0:T(8,128)(2,1)S(1)}, u32[]{:S(2)}, u32[]{:S(2)}) %collective-permute-start) | collective-permute-done | bytes 262176 | tf_op jit(solution)/shard_map/ppermute | solution.py:14
  353.4 1.7 collective-permute-start.1
  355.1 0.9 fusion.38
  356.0 0.9 fusion.37
  356.8 1.1 collective-permute-start.2
  357.9 4.0 collective-permute-done.1
  362.0 2.1 collective-permute-done.2
  364.2 0.3 convolution_bitcast_fusion.2
  364.5 0.3 convolution_bitcast_fusion.1
  364.8 0.7 pad_maximum_fusion.1
  365.6 0.6 subtract_reduce_fusion
  366.2 124.8 %psum.36 = f32[]{:T(128)} all-reduce(f32[]{:T(128)} %subtract_reduce_fusion), channel_id=1, replica_groups=mesh['node'=64,'feat'=4] {'node'}, use_global_device_ids=true, to_apply=%region_6.7 | all-reduce | flops 1 | bytes 8 | tf_op jit(solution)/shard_map/psum | solution.py:106
  491.6 54.8 %all-reduce.6.cloned.1.call-done = (f32[2,32,1024]{2,1,0:T(8,128)}, f32[256,172]{0,1:T(8,128)}, f32[256,172]{0,1:T(8,128)}) async-done(((f32[2,32,1024]{2,1,0:T(8,128)}, f32[256,172]{0,1:T(8,128)}, f32[256,172]{0,1:T(8,128)}), (f32[2,32,1024]{2,1,0:T(8,128)}, f32[256,172]{0,1:T(8,128)}, f32[256,172]{0,1:T(8,128)})) %all-reduce.6.cloned.1.call-update) | async-done | bytes 614416 | tf_op jit(solution)/shard_map/psum | solution.py:137
  546.5 1.7 slice_bitcast_fusion
  548.1 1.6 copy.71
  549.7 1.6 copy.72
  (49 shorter events, 0.8 us)
Async XLA Ops:
  7.2 44.1 %copy-start = (bf16[4,16,128,128]{3,2,1,0:T(8,128)(2,1)S(1)}, bf16[4,16,128,128]{3,2,1,0:T(8,128)(2,1)}, u32[]{:S(2)}) copy-start(bf16[4,16,128,128]{3,2,1,0:T(8,128)(2,1)} %param.14) | copy-start | bytes 6291460
  22.1 15.5 %copy-start.11 = (s32[4,16]{1,0:T(4,128)S(1)}, s32[4,16]{1,0:T(4,128)}, u32[]{:S(2)}) copy-start(s32[4,16]{1,0:T(4,128)} %param.13) | copy-start | bytes 772
  22.1 15.6 %copy-start.5 = (bf16[512,32]{0,1:T(8,128)(2,1)S(1)}, bf16[512,32]{0,1:T(8,128)(2,1)}, u32[]{:S(2)}) copy-start(bf16[512,32]{0,1:T(8,128)(2,1)} %param.10) | copy-start | bytes 98308
  22.1 15.6 %copy-start.10 = (bf16[32,1024]{1,0:T(8,128)(2,1)S(1)}, bf16[32,1024]{1,0:T(8,128)(2,1)}, u32[]{:S(2)}) copy-start(bf16[32,1024]{1,0:T(8,128)(2,1)} %param.16) | copy-start | bytes 196612
  25.4 24.1 %all-to-all-start = ((bf16[64,2,1024]{2,1,0:T(2,128)(2,1)}), bf16[64,2,1024]{2,1,0:T(2,128)(2,1)S(1)}, u32[]{:S(2)}, u32[]{:S(2)}) async-start(bf16[64,2,1024]{2,1,0:T(2,128)(2,1)} %reshape.178), calls=%async_computation | async-start | bytes 524288 | tf_op jit(solution)/shard_map/all_to_all | solution.py:87
  37.5 45.1 %reduce-scatter.2.cloned.1.call-start = ((), (), s32[]{:S(2)}) async-start(), calls=%async_computation.4 | async-start | bytes 2621440 | tf_op jit(solution)/shard_map/reduce_scatter | solution.py:93
  51.3 1.6 copy-start.3
  51.3 1.6 copy-start.9
  105.2 10.9 %copy-start.7 = (bf16[256,172]{0,1:T(8,128)(2,1)S(1)}, bf16[256,172]{0,1:T(8,128)(2,1)}, u32[]{:S(2)}) copy-start(bf16[256,172]{0,1:T(8,128)(2,1)} %param.18) | copy-start | bytes 264196
  105.2 61.9 %all-to-all-start.1 = ((bf16[64,64,256]{2,1,0:T(8,128)(2,1)}), bf16[64,64,256]{2,1,0:T(8,128)(2,1)}, u32[]{:S(2)}, u32[]{:S(2)}) async-start(bf16[64,64,256]{2,1,0:T(8,128)(2,1)} %select_select_fusion), calls=%async_computation.2 | async-start | bytes 4194304 | tf_op jit(solution)/shard_map/all_to_all | solution.py:98
  116.1 105.6 %all-reduce.4.cloned.1.call-start = ((), (), s32[]{:S(2)}) async-start(), calls=%async_computation.5 | async-start | bytes 720896 | tf_op jit(solution)/shard_map/psum | solution.py:104
  174.7 3.2 copy-start.6
  174.7 48.0 %copy-start.12 = (s32[512]{0:T(512)S(1)}, s32[512]{0:T(512)}, u32[]{:S(2)}) copy-start(s32[512]{0:T(512)} %param.15) | copy-start | bytes 6148
  250.8 2.3 copy-start.2
  255.9 10.9 %copy-start.8 = (s32[1,64,64]{2,1,0:T(8,128)S(1)}, s32[1,64,64]{2,1,0:T(8,128)}, u32[]{:S(2)}) copy-start(s32[1,64,64]{2,1,0:T(8,128)} %param.11) | copy-start | bytes 49156
  255.9 11.0 %slice-start = ((f32[36,32768]{1,0:T(8,128)}), f32[4,32768]{1,0:T(4,128)S(1)}, s32[]{:S(2)}) async-start(f32[36,32768]{1,0:T(8,128)} %copy-done.2), calls=%async_computation.7 | async-start | bytes 1048576 | tf_op jit(solution)/shard_map/slice | solution.py:128
  255.9 61.9 %all-to-all-start.2 = ((bf16[64,64,256]{2,1,0:T(8,128)(2,1)}), bf16[64,64,256]{2,1,0:T(8,128)(2,1)}, u32[]{:S(2)}, u32[]{:S(2)}) async-start(bf16[64,64,256]{2,1,0:T(8,128)(2,1)} %convert_element_type.51), calls=%async_computation.3 | async-start | bytes 4194304 | tf_op jit(solution)/shard_map/all_to_all | solution.py:120
  266.7 279.7 %all-reduce.6.cloned.1.call-start = ((), (), s32[]{:S(2)}) async-start(), calls=%async_computation.6 | async-start | bytes 1245184 | tf_op jit(solution)/shard_map/psum | solution.py:137
  321.3 23.3 %copy-start.4 = (f32[512,256]{1,0:T(8,128)S(1)}, f32[512,256]{1,0:T(8,128)}, u32[]{:S(2)}) copy-start(f32[512,256]{1,0:T(8,128)} %reduce-scatter.2.cloned.1.call-done) | copy-start | bytes 1572868
  345.0 8.4 %collective-permute-start = (bf16[512,256]{1,0:T(8,128)(2,1)S(1)}, bf16[512,256]{1,0:T(8,128)(2,1)S(1)}, u32[]{:S(2)}, u32[]{:S(2)}) collective-permute-start(bf16[512,256]{1,0:T(8,128)(2,1)S(1)} %fusion.20), channel_id=1, source_target_pairs={{0,1},{1,2},{2,3},{3,0},{4,5},{5,6},{6,7},{7,4},{8,9},{9,10},{10,1... | collective-permute-start | bytes 786440 | tf_op jit(solution)/shard_map/ppermute | solution.py:14
  353.4 8.5 %collective-permute-start.1 = (bf16[512,256]{1,0:T(8,128)(2,1)S(1)}, bf16[512,256]{1,0:T(8,128)(2,1)S(1)}, u32[]{:S(2)}, u32[]{:S(2)}) collective-permute-start(bf16[512,256]{1,0:T(8,128)(2,1)S(1)} %collective-permute-done), channel_id=1, source_target_pairs={{0,1},{1,2},{2,3},{3,0},{4,5},{5,6},{6,7},{7,4},{8,9},{9,10},{10,1... | collective-permute-start | bytes 786440 | tf_op jit(solution)/shard_map/ppermute | solution.py:14
  356.8 7.2 %collective-permute-start.2 = (bf16[512,256]{1,0:T(8,128)(2,1)S(1)}, bf16[512,256]{1,0:T(8,128)(2,1)S(1)}, u32[]{:S(2)}, u32[]{:S(2)}) collective-permute-start(bf16[512,256]{1,0:T(8,128)(2,1)S(1)} %fusion.20), channel_id=1, source_target_pairs={{0,3},{1,0},{2,1},{3,2},{4,7},{5,4},{6,5},{7,6},{8,11},{9,8},{10,9... | collective-permute-start | bytes 786440 | tf_op jit(solution)/shard_map/ppermute | solution.py:16
  364.2 187.1 %copy-start.1 = (bf16[4,16,128,128]{3,2,1,0:T(8,128)(2,1)S(1)}, bf16[4,16,128,128]{3,2,1,0:T(8,128)(2,1)}, u32[]{:S(2)}) copy-start(bf16[4,16,128,128]{3,2,1,0:T(8,128)(2,1)} %param.14) | copy-start | bytes 6291460
Sparse Core Ops, SparseCore 0:
  54.8 27.8 reduce-scatter.1
  179.1 42.5 all-reduce.3
  365.7 180.7 all-reduce.5
